TPU v7x, 32 devices: a whole 2x2x4 slice. The times are simulated.
32 devices in a mesh: grp: 2 (over x), con: 16 (over z, y, core).
Axes of the slice: x: 2, y: 2, z: 4, core: 2. Of those that a mesh axis runs over, the one named last changes fastest.
Arguments:
- matrix: float32 [32768, 2048], P(('grp', 'con')), parts along dimension 0, may hold values from -0.046875 to 0.046875
- bounds_rhs: float32 [32768, 128], P(('grp', 'con')), parts along dimension 0, may hold values from -3 to 3
- costs: float32 [4096, 128], P(('grp', 'con')), parts along dimension 0, may hold values from -12 to 12
- upper: float32 [4096], P(('grp', 'con')), parts along dimension 0, may hold values from 0.5 to 2
- bound_mask: int32 [4096], P(('grp', 'con')), parts along dimension 0, may hold values 0 or 1
- node_map: int32 [3, 256], P(None, 'grp'), parts along dimension 1, may hold values from 0 to 63, as said below
- weights: int32 [256], P('grp'), parts along dimension 0, may hold values from 1 to 10
Outputs:
- primal: float32 [4096, 128], P(('grp', 'con')), parts along dimension 0
- dual: float32 [32768, 128], P(('grp', 'con')), parts along dimension 0
- multipliers: float32 [4096, 128], P(('grp', 'con')), parts along dimension 0
- gaps: float32 [4], P('grp'), parts along dimension 0
There are 2 independent parts, one for each index of `grp`. A program takes and returns all parts, laid end to end along the dimension named above; each array names one. Nothing has to cross between parts.
Inputs may be any that keep to these rules, and one draw needn't show every extreme that they name: `node_map`: row t numbers the 4 ** (t + 1) nodes of that section; each node holds 128 / 4 ** (t + 1) scenarios, and the nodes of row t + 1 split those of row t.
All inputs are finite; a program needn't handle non-finite values. No bound on the sum of `bound_mask` on one device may be relied on, other than what follows from the above.
Results may differ from a plain program's by a relative error of at most 0.0001.
Values sent between devices are 32-bit elements; how exact they have to be, the bound alone decides.
A program may use at most 64 MiB of HBM per device.

v0:
```python
import jax
import jax.numpy as jnp
from jax import lax
from jax.sharding import PartitionSpec as P

N = 2048
OUTER = 2
INNER = 2


highest = lax.Precision.HIGHEST
step_primal = 0.4
step_dual = 0.6
penalty = 1.0


def node_average(node_map, weights):
    weight_float = weights.astype(jnp.float32)
    probability = weight_float / jnp.sum(weight_float)
    same_node = (node_map[:, :, None] == node_map[:, None, :]).astype(jnp.float32)
    node_mass = same_node * probability[None, None, :]
    return (node_mass / jnp.sum(node_mass, axis=2, keepdims=True), probability)


def consensus(primal, averaging, column_index):
    averaged = jnp.einsum("tsr,jr->tjs", averaging, primal, precision=highest)
    section_of = column_index % (averaging.shape[0] + 1)
    section_hot = (
        section_of[None, :] == jnp.arange(averaging.shape[0], dtype=jnp.int32)[:, None]
    ).astype(jnp.float32)
    free_cols = 1.0 - jnp.sum(section_hot, axis=0)
    return jnp.sum(section_hot[:, :, None] * averaged, axis=0) + free_cols[:, None] * primal


def primal_step(primal, costs, multipliers, average, transposed, upper, flags, prox_weight):
    gradient = costs + multipliers + prox_weight * (primal - average) + transposed
    moved = jnp.maximum(primal - step_primal * gradient, 0.0)
    return jnp.where(flags[:, None] > 0, jnp.minimum(moved, upper[:, None]), moved)


def apply_rows(matrix, extrap):
    return jnp.dot(matrix, lax.all_gather(extrap, "con", axis=0, tiled=True), precision=highest)


def apply_columns(matrix, dual):
    return lax.psum_scatter(
        lax.dot_general(matrix, dual, (((0,), (0,)), ((), ())), precision=highest),
        "con",
        scatter_dimension=0,
        tiled=True,
    )


def body(matrix, bounds_rhs, costs, upper, bound_mask, node_map, weights):
    own_cols = costs.shape[0]
    scenario_count = costs.shape[1]
    averaging, probability = node_average(node_map, weights)
    start_col = lax.axis_index("con") * own_cols
    costs_all, upper_all, flags_all = (costs, upper, bound_mask.astype(jnp.float32))
    width = costs_all.shape[0]
    column_index = start_col + jnp.arange(width, dtype=jnp.int32)
    primal = jnp.zeros((width, scenario_count), jnp.float32)
    multipliers = jnp.zeros((width, scenario_count), jnp.float32)
    average = jnp.zeros((width, scenario_count), jnp.float32)
    transposed = jnp.zeros((width, scenario_count), jnp.float32)
    dual = jnp.zeros(bounds_rhs.shape, jnp.float32)
    partials = []
    for outer_turn in range(OUTER):
        prox_weight = 0.0 if outer_turn == 0 else penalty
        for inner_turn in range(INNER):
            moved = primal_step(
                primal,
                costs_all,
                multipliers,
                average,
                transposed,
                upper_all,
                flags_all,
                prox_weight,
            )
            extrap = 2.0 * moved - primal
            product = apply_rows(matrix, extrap)
            dual = jnp.maximum(dual + step_dual * (product - bounds_rhs), 0.0)
            primal = moved
            if outer_turn < OUTER - 1 or inner_turn < INNER - 1:
                transposed = apply_columns(matrix, dual)
        average = consensus(primal, averaging, column_index)
        deviation = primal - average
        multipliers = multipliers + penalty * deviation
        partial_value = jnp.sum(deviation * deviation * probability[None, :]) / N
        partial_value = lax.psum(partial_value, "con")
        partials.append(partial_value)
    gaps = jnp.stack(partials)
    return (primal, dual, multipliers, gaps)


def solution(mesh):
    placed = (
        P(("grp", "con"), None),
        P(("grp", "con"), None),
        P(("grp", "con"), None),
        P(("grp", "con")),
        P(("grp", "con")),
        P(None, "grp"),
        P("grp"),
    )
    return jax.shard_map(
        body,
        mesh=mesh,
        in_specs=placed,
        out_specs=(
            P(("grp", "con"), None),
            P(("grp", "con"), None),
            P(("grp", "con"), None),
            P("grp"),
        ),
        check_vma=False,
    )
```

profile of v0, /device:TPU:0, one launch (start us, length us, event | category | flops | bytes accessed | tf_op | source)
XLA Modules:
  0.0 413.3 jit_solution(4604648816111772595)
XLA Ops:
  7.2 0.0 all-gather.5.cloned.1.call-start
  7.2 0.7 convert_compare_fusion
  7.9 0.9 copy.23
  8.8 1.3 fusion.31
  10.1 0.0 all-gather.5.cloned.1.call-update
  10.1 0.0 reduce-scatter.4.cloned.1.call-start
  10.2 1.2 copy.25
  11.4 0.0 copy-start.2
  11.4 38.8 %all-gather.5.cloned.1.call-done = f32[2048,128]{0,1:T(8,128)} async-done(((f32[128,128]{0,1:T(8,128)}), f32[2048,128]{0,1:T(8,128)}) %all-gather.5.cloned.1.call-update) | async-done | bytes 1048592 | tf_op jit(solution)/shard_map/all_gather | solution.py:42
  50.3 12.0 %fusion.8 = f32[1024,128]{0,1:T(8,128)S(1)} fusion(f32[1024,128]{0,1:T(8,128)S(1)} %copy.25, f32[2048,128]{0,1:T(8,128)} %all-gather.5.cloned.1.call-done, f32[1024,2048]{1,0:T(8,128)} %param.7), kind=kOutput, calls=%fused_computation.15 | convolution fusion | flops 3221618688 | bytes 10485760 | tf_op jit(solution)/shard_map/dot_general | solution.py:42
  62.3 5.6 %convolution_bitcast_fusion.2 = f32[2048,128]{0,1:T(8,128)} fusion(f32[1024,128]{0,1:T(8,128)S(1)} %fusion.8, f32[1024,2048]{1,0:T(8,128)S(1)} %copy-done), kind=kOutput, calls=%fused_computation.2 | convolution fusion | flops 3221225472 | bytes 9961472 | tf_op jit(solution)/shard_map/dot_general | solution.py:47
  67.8 0.0 reduce-scatter.4.cloned.1.call-update
  67.9 0.0 all-gather.7.cloned.1.call-start
  67.9 57.0 %reduce-scatter.4.cloned.1.call-done = f32[128,128]{0,1:T(8,128)} async-done(((f32[2048,128]{0,1:T(8,128)}), f32[128,128]{0,1:T(8,128)}) %reduce-scatter.4.cloned.1.call-update) | async-done | bytes 65552 | tf_op jit(solution)/shard_map/reduce_scatter | solution.py:46
  124.9 1.5 multiply_subtract_fusion.2
  126.5 0.0 all-gather.7.cloned.1.call-update
  126.5 0.2 reduce-scatter.6.cloned.1.call-start
  126.7 37.0 %all-gather.7.cloned.1.call-done = f32[2048,128]{0,1:T(8,128)} async-done(((f32[128,128]{0,1:T(8,128)}), f32[2048,128]{0,1:T(8,128)}) %all-gather.7.cloned.1.call-update) | async-done | bytes 1048592 | tf_op jit(solution)/shard_map/all_gather | solution.py:42
  163.7 11.5 %fusion.10 = f32[1024,128]{0,1:T(8,128)S(1)} fusion(f32[1024,128]{0,1:T(8,128)S(1)} %fusion.8, f32[1024,128]{0,1:T(8,128)S(1)} %copy.25, f32[2048,128]{0,1:T(8,128)} %all-gather.7.cloned.1.call-done, f32[1024,2048]{1,0:T(8,128)} %param.7), kind=kOutput, calls=%fused_computation.17 | convolution fusion | flops 3221749760 | bytes 11010048 | tf_op jit(solution)/shard_map/dot_general | solution.py:42
  175.2 7.8 %convolution_bitcast_fusion.1 = f32[2048,128]{0,1:T(8,128)} fusion(f32[1024,128]{0,1:T(8,128)S(1)} %fusion.10, f32[1024,2048]{1,0:T(8,128)} %param.7), kind=kOutput, calls=%fused_computation.1 | convolution fusion | flops 3221225472 | bytes 9961472 | tf_op jit(solution)/shard_map/dot_general | solution.py:47
  183.0 0.0 reduce-scatter.6.cloned.1.call-update
  183.1 0.0 all-gather.9.cloned.1.call-start
  183.1 0.6 convert_reduce_fusion
  183.8 0.6 convert_divide_fusion
  184.4 0.2 select_reduce_fusion
  184.7 0.5 fusion.17
  185.2 0.1 copy.27
  185.3 54.8 %reduce-scatter.6.cloned.1.call-done = f32[128,128]{0,1:T(8,128)} async-done(((f32[2048,128]{0,1:T(8,128)}), f32[128,128]{0,1:T(8,128)}) %reduce-scatter.6.cloned.1.call-update) | async-done | bytes 65552 | tf_op jit(solution)/shard_map/reduce_scatter | solution.py:46
  240.1 1.5 multiply_subtract_fusion.1
  241.6 0.0 all-gather.9.cloned.1.call-update
  241.6 0.3 reduce-scatter.8.cloned.1.call-start
  241.9 36.7 %all-gather.9.cloned.1.call-done = f32[2048,128]{0,1:T(8,128)} async-done(((f32[128,128]{0,1:T(8,128)}), f32[2048,128]{0,1:T(8,128)}) %all-gather.9.cloned.1.call-update) | async-done | bytes 1048592 | tf_op jit(solution)/shard_map/all_gather | solution.py:42
  278.6 11.4 %fusion.12 = f32[1024,128]{0,1:T(8,128)S(1)} fusion(f32[1024,128]{0,1:T(8,128)S(1)} %fusion.10, f32[1024,128]{0,1:T(8,128)S(1)} %copy.25, f32[2048,128]{0,1:T(8,128)} %all-gather.9.cloned.1.call-done, f32[1024,2048]{1,0:T(8,128)} %param.7), kind=kOutput, calls=%fused_computation.19 | convolution fusion | flops 3221749760 | bytes 11010048 | tf_op jit(solution)/shard_map/dot_general | solution.py:42
  290.0 7.8 %convolution_bitcast_fusion = f32[2048,128]{0,1:T(8,128)} fusion(f32[1024,128]{0,1:T(8,128)S(1)} %fusion.12, f32[1024,2048]{1,0:T(8,128)} %param.7), kind=kOutput, calls=%fused_computation | convolution fusion | flops 3221225472 | bytes 9961472 | tf_op jit(solution)/shard_map/dot_general | solution.py:47
  297.9 0.0 reduce-scatter.8.cloned.1.call-update
  297.9 0.0 all-gather.11.cloned.1.call-start
  297.9 57.0 %reduce-scatter.8.cloned.1.call-done = f32[128,128]{0,1:T(8,128)} async-done(((f32[2048,128]{0,1:T(8,128)}), f32[128,128]{0,1:T(8,128)}) %reduce-scatter.8.cloned.1.call-update) | async-done | bytes 65552 | tf_op jit(solution)/shard_map/reduce_scatter | solution.py:46
  355.0 1.5 multiply_subtract_fusion
  356.5 0.0 all-gather.11.cloned.1.call-update
  356.5 0.5 fusion.18
  357.0 0.1 copy.33
  357.1 0.7 multiply_reduce_fusion.1
  359.1 31.6 %all-reduce = (f32[1]{0:T(128)}, f32[1]{0:T(128)}) all-reduce(f32[1]{0:T(128)} %bitcast.12, f32[1]{0:T(128)} %bitcast.11), channel_id=1, replica_groups=mesh['grp'=2,'con'=16] {'con'}, use_global_device_ids=true, to_apply=%region_11.12 | all-reduce | flops 2 | bytes 16 | tf_op jit(solution)/shard_map/psum | solution.py:91
  390.7 0.7 copy.34
  391.4 0.7 copy.36
  392.2 1.8 pad_maximum_fusion
  394.0 11.5 %fusion.14 = f32[1024,128]{0,1:T(8,128)S(1)} fusion(f32[1024,128]{0,1:T(8,128)S(1)} %fusion.12, f32[1024,128]{0,1:T(8,128)S(1)} %copy.25, f32[2048,128]{0,1:T(8,128)} %all-gather.11.cloned.1.call-done, f32[1024,2048]{1,0:T(8,128)} %param.7), kind=kOutput, calls=%fused_computation.21 | convolution fusion | flops 3221749760 | bytes 11010048 | tf_op jit(solution)/shard_map/dot_general | solution.py:42
  405.5 1.0 copy.35
  (12 shorter events, 0.1 us)
Async XLA Ops:
  7.2 43.1 %all-gather.5.cloned.1.call-start = ((), (), s32[]{:S(2)}) async-start(), calls=%async_computation.3 | async-start | bytes 1114112 | tf_op jit(solution)/shard_map/all_gather | solution.py:42
  10.1 114.8 %reduce-scatter.4.cloned.1.call-start = ((), (), s32[]{:S(2)}) async-start(), calls=%async_computation.4 | async-start | bytes 1114112 | tf_op jit(solution)/shard_map/reduce_scatter | solution.py:46
  11.4 113.5 %copy-start.2 = (f32[128]{0:T(128)S(1)}, f32[128]{0:T(128)}, u32[]{:S(2)}) copy-start(f32[128]{0:T(128)} %param.10) | copy-start | bytes 1540
  50.3 12.0 %copy-start = (f32[1024,2048]{1,0:T(8,128)S(1)}, f32[1024,2048]{1,0:T(8,128)}, u32[]{:S(2)}) copy-start(f32[1024,2048]{1,0:T(8,128)} %param.7) | copy-start | bytes 25165828
  67.9 95.9 %all-gather.7.cloned.1.call-start = ((), (), s32[]{:S(2)}) async-start(), calls=%async_computation.5 | async-start | bytes 1114112 | tf_op jit(solution)/shard_map/all_gather | solution.py:42
  126.5 56.7 %copy-start.3 = (s32[128]{0:T(128)S(1)}, s32[128]{0:T(128)}, u32[]{:S(2)}) copy-start(s32[128]{0:T(128)} %param.13) | copy-start | bytes 1540
  126.5 57.9 %copy-start.1 = (s32[3,128]{1,0:T(4,128)S(1)}, s32[3,128]{1,0:T(4,128)}, u32[]{:S(2)}) copy-start(s32[3,128]{1,0:T(4,128)} %param.12) | copy-start | bytes 4612
  126.5 113.6 %reduce-scatter.6.cloned.1.call-start = ((), (), s32[]{:S(2)}) async-start(), calls=%async_computation.6 | async-start | bytes 1114112 | tf_op jit(solution)/shard_map/reduce_scatter | solution.py:46
  183.1 95.5 %all-gather.9.cloned.1.call-start = ((), (), s32[]{:S(2)}) async-start(), calls=%async_computation.7 | async-start | bytes 1114112 | tf_op jit(solution)/shard_map/all_gather | solution.py:42
  241.6 113.4 %reduce-scatter.8.cloned.1.call-start = ((), (), s32[]{:S(2)}) async-start(), calls=%async_computation.8 | async-start | bytes 1114112 | tf_op jit(solution)/shard_map/reduce_scatter | solution.py:46
  297.9 96.1 %all-gather.11.cloned.1.call-start = ((), (), s32[]{:S(2)}) async-start(), calls=%async_computation.9 | async-start | bytes 1114112 | tf_op jit(solution)/shard_map/all_gather | solution.py:42
Sparse Core Ops, SparseCore 0:
  10.7 39.4 all-gather.4
  68.0 56.8 reduce-scatter.3
  127.9 35.7 all-gather.6
  183.2 56.8 reduce-scatter.5
  242.7 35.8 all-gather.8
  298.0 56.9 reduce-scatter.7
  357.9 35.7 all-gather.10
where the time goes:
time: 414 us; the launch traced here: 413 us
  waiting for transfers between devices  281 us (68%)
  matrix products  68.6 us (17%)
  blocking collectives  31.6 us (8%)
  between operations  15.6 us (4%)
  other arithmetic  10.5 us (3%)
  local copies, waits for them, and re-layouts  4.82 us (1%)
    reduce_scatter x3, waiting for transfers between devices, apply_columns(): lax.psum_scatter(lax.dot_general(matrix, dual, (((0,), (0,)), ((), ())),...  169 us
    all_gather x4, waiting for transfers between devices, apply_rows(): lax.all_gather(extrap, 'con', axis=0, tiled=True)  112 us
    dot_general x4, matrix products, apply_rows(): jnp.dot(matrix, lax.all_gather(extrap, 'con', axis=0, tiled=True), precis...  46.4 us
    psum x1, blocking collectives, body(): partial_value = lax.psum(partial_value, 'con')  31.6 us
    dot_general x3, matrix products, apply_columns(): lax.dot_general(matrix, dual, (((0,), (0,)), ((), ())), precision=highest)  21.3 us
  transfers between devices with their start and end apart: 7, of which 6 were waited for; matrix products, arithmetic and copies ran while one was open for 2% of the time, Pallas kernels for 0%

commit v1 on v0

--- a/solution.py
+++ b/solution.py
@@ -39,12 +39,12 @@
 
 
 def apply_rows(matrix, extrap):
-    return jnp.dot(matrix, lax.all_gather(extrap, "con", axis=0, tiled=True), precision=highest)
+    return jnp.dot(matrix, lax.all_gather(extrap, "con", axis=0, tiled=True), precision=lax.Precision.HIGH)
 
 
 def apply_columns(matrix, dual):
     return lax.psum_scatter(
-        lax.dot_general(matrix, dual, (((0,), (0,)), ((), ())), precision=highest),
+        lax.dot_general(matrix, dual, (((0,), (0,)), ((), ())), precision=lax.Precision.HIGH),
         "con",
         scatter_dimension=0,
         tiled=True,

time: 414 us -> 397 us (0.959)
  matrix products: 68.6 us -> 51.4 us
    dot_general x4, matrix products: 46.4 us -> 32 us  [apply_rows(): jnp.dot(matrix, lax.all_gather(extrap, 'con', axis=0, tiled=True), precis...]
where the time goes in v1:
time: 397 us; the launch traced here: 396 us
  waiting for transfers between devices  281 us (71%)
  matrix products  51.4 us (13%)
  blocking collectives  31.6 us (8%)
  between operations  15.6 us (4%)
  other arithmetic  10.5 us (3%)
  local copies, waits for them, and re-layouts  4.82 us (1%)
    reduce_scatter x3, waiting for transfers between devices, apply_columns(): lax.psum_scatter(lax.dot_general(matrix, dual, (((0,), (0,)), ((), ())),...  169 us
    all_gather x4, waiting for transfers between devices, apply_rows(): lax.all_gather(extrap, 'con', axis=0, tiled=True)  112 us
    dot_general x4, matrix products, apply_rows(): jnp.dot(matrix, lax.all_gather(extrap, 'con', axis=0, tiled=True), precis...  32 us
    psum x1, blocking collectives, body(): partial_value = lax.psum(partial_value, 'con')  31.6 us
    dot_general x3, matrix products, apply_columns(): lax.dot_general(matrix, dual, (((0,), (0,)), ((), ())), precision=lax.Pre...  18.3 us
  transfers between devices with their start and end apart: 7, of which 6 were waited for; matrix products, arithmetic and copies ran while one was open for 2% of the time, Pallas kernels for 0%

profile of v1, /device:TPU:0, one launch (start us, length us, event | category | flops | bytes accessed | tf_op | source)
XLA Modules:
  0.0 396.0 jit_solution(430847852660730652)
XLA Ops:
  7.2 0.0 all-gather.5.cloned.1.call-start
  7.2 0.7 convert_compare_fusion
  7.9 0.9 copy.23
  8.8 1.3 fusion.31
  10.1 0.0 all-gather.5.cloned.1.call-update
  10.1 0.0 reduce-scatter.4.cloned.1.call-start
  10.2 1.2 copy.25
  11.4 38.8 %all-gather.5.cloned.1.call-done = f32[2048,128]{0,1:T(8,128)} async-done(((f32[128,128]{0,1:T(8,128)}), f32[2048,128]{0,1:T(8,128)}) %all-gather.5.cloned.1.call-update) | async-done | bytes 1048592 | tf_op jit(solution)/shard_map/all_gather | solution.py:42
  50.3 8.1 %fusion.8 = f32[1024,128]{0,1:T(8,128)S(1)} fusion(f32[1024,128]{0,1:T(8,128)S(1)} %copy.25, f32[2048,128]{0,1:T(8,128)} %all-gather.5.cloned.1.call-done, f32[1024,2048]{1,0:T(8,128)} %param.7), kind=kOutput, calls=%fused_computation.15 | convolution fusion | flops 1611005952 | bytes 10485760 | tf_op jit(solution)/shard_map/dot_general | solution.py:42
  58.4 4.3 %convolution_bitcast_fusion.2 = f32[2048,128]{0,1:T(8,128)} fusion(f32[1024,128]{0,1:T(8,128)S(1)} %fusion.8, f32[1024,2048]{1,0:T(8,128)S(1)} %copy-done), kind=kOutput, calls=%fused_computation.2 | convolution fusion | flops 1610612736 | bytes 9961472 | tf_op jit(solution)/shard_map/dot_general | solution.py:47
  62.6 0.0 reduce-scatter.4.cloned.1.call-update
  62.7 0.0 all-gather.7.cloned.1.call-start
  62.7 57.0 %reduce-scatter.4.cloned.1.call-done = f32[128,128]{0,1:T(8,128)} async-done(((f32[2048,128]{0,1:T(8,128)}), f32[128,128]{0,1:T(8,128)}) %reduce-scatter.4.cloned.1.call-update) | async-done | bytes 65552 | tf_op jit(solution)/shard_map/reduce_scatter | solution.py:46
  119.7 1.5 multiply_subtract_fusion.2
  121.2 0.0 all-gather.7.cloned.1.call-update
  121.3 0.0 copy-start.3
  121.3 0.2 reduce-scatter.6.cloned.1.call-start
  121.5 37.0 %all-gather.7.cloned.1.call-done = f32[2048,128]{0,1:T(8,128)} async-done(((f32[128,128]{0,1:T(8,128)}), f32[2048,128]{0,1:T(8,128)}) %all-gather.7.cloned.1.call-update) | async-done | bytes 1048592 | tf_op jit(solution)/shard_map/all_gather | solution.py:42
  158.5 8.0 %fusion.10 = f32[1024,128]{0,1:T(8,128)S(1)} fusion(f32[1024,128]{0,1:T(8,128)S(1)} %fusion.8, f32[1024,128]{0,1:T(8,128)S(1)} %copy.25, f32[2048,128]{0,1:T(8,128)} %all-gather.7.cloned.1.call-done, f32[1024,2048]{1,0:T(8,128)} %param.7), kind=kOutput, calls=%fused_computation.17 | convolution fusion | flops 1611137024 | bytes 11010048 | tf_op jit(solution)/shard_map/dot_general | solution.py:42
  166.5 7.0 %convolution_bitcast_fusion.1 = f32[2048,128]{0,1:T(8,128)} fusion(f32[1024,128]{0,1:T(8,128)S(1)} %fusion.10, f32[1024,2048]{1,0:T(8,128)} %param.7), kind=kOutput, calls=%fused_computation.1 | convolution fusion | flops 1610612736 | bytes 9961472 | tf_op jit(solution)/shard_map/dot_general | solution.py:47
  173.5 0.0 reduce-scatter.6.cloned.1.call-update
  173.6 0.0 all-gather.9.cloned.1.call-start
  173.6 0.6 convert_reduce_fusion
  174.3 0.6 convert_divide_fusion
  174.9 0.2 select_reduce_fusion
  175.2 0.5 fusion.17
  175.7 0.1 copy.27
  175.8 54.8 %reduce-scatter.6.cloned.1.call-done = f32[128,128]{0,1:T(8,128)} async-done(((f32[2048,128]{0,1:T(8,128)}), f32[128,128]{0,1:T(8,128)}) %reduce-scatter.6.cloned.1.call-update) | async-done | bytes 65552 | tf_op jit(solution)/shard_map/reduce_scatter | solution.py:46
  230.6 1.5 multiply_subtract_fusion.1
  232.1 0.0 all-gather.9.cloned.1.call-update
  232.1 0.3 reduce-scatter.8.cloned.1.call-start
  232.4 36.6 %all-gather.9.cloned.1.call-done = f32[2048,128]{0,1:T(8,128)} async-done(((f32[128,128]{0,1:T(8,128)}), f32[2048,128]{0,1:T(8,128)}) %all-gather.9.cloned.1.call-update) | async-done | bytes 1048592 | tf_op jit(solution)/shard_map/all_gather | solution.py:42
  269.1 8.0 %fusion.12 = f32[1024,128]{0,1:T(8,128)S(1)} fusion(f32[1024,128]{0,1:T(8,128)S(1)} %fusion.10, f32[1024,128]{0,1:T(8,128)S(1)} %copy.25, f32[2048,128]{0,1:T(8,128)} %all-gather.9.cloned.1.call-done, f32[1024,2048]{1,0:T(8,128)} %param.7), kind=kOutput, calls=%fused_computation.19 | convolution fusion | flops 1611137024 | bytes 11010048 | tf_op jit(solution)/shard_map/dot_general | solution.py:42
  277.0 7.0 %convolution_bitcast_fusion = f32[2048,128]{0,1:T(8,128)} fusion(f32[1024,128]{0,1:T(8,128)S(1)} %fusion.12, f32[1024,2048]{1,0:T(8,128)} %param.7), kind=kOutput, calls=%fused_computation | convolution fusion | flops 1610612736 | bytes 9961472 | tf_op jit(solution)/shard_map/dot_general | solution.py:47
  284.1 0.0 reduce-scatter.8.cloned.1.call-update
  284.1 0.0 all-gather.11.cloned.1.call-start
  284.1 57.0 %reduce-scatter.8.cloned.1.call-done = f32[128,128]{0,1:T(8,128)} async-done(((f32[2048,128]{0,1:T(8,128)}), f32[128,128]{0,1:T(8,128)}) %reduce-scatter.8.cloned.1.call-update) | async-done | bytes 65552 | tf_op jit(solution)/shard_map/reduce_scatter | solution.py:46
  341.1 1.5 multiply_subtract_fusion
  342.6 0.0 all-gather.11.cloned.1.call-update
  342.6 0.5 fusion.18
  343.1 0.1 copy.33
  343.2 0.7 multiply_reduce_fusion.1
  345.2 31.6 %all-reduce = (f32[1]{0:T(128)}, f32[1]{0:T(128)}) all-reduce(f32[1]{0:T(128)} %bitcast.12, f32[1]{0:T(128)} %bitcast.11), channel_id=1, replica_groups=mesh['grp'=2,'con'=16] {'con'}, use_global_device_ids=true, to_apply=%region_11.12 | all-reduce | flops 2 | bytes 16 | tf_op jit(solution)/shard_map/psum | solution.py:91
  376.9 0.7 copy.34
  377.6 0.7 copy.36
  378.3 1.8 pad_maximum_fusion
  380.2 8.0 %fusion.14 = f32[1024,128]{0,1:T(8,128)S(1)} fusion(f32[1024,128]{0,1:T(8,128)S(1)} %fusion.12, f32[1024,128]{0,1:T(8,128)S(1)} %copy.25, f32[2048,128]{0,1:T(8,128)} %all-gather.11.cloned.1.call-done, f32[1024,2048]{1,0:T(8,128)} %param.7), kind=kOutput, calls=%fused_computation.21 | convolution fusion | flops 1611137024 | bytes 11010048 | tf_op jit(solution)/shard_map/dot_general | solution.py:42
  388.1 1.0 copy.35
  (12 shorter events, 0.1 us)
Async XLA Ops:
  7.2 43.1 %all-gather.5.cloned.1.call-start = ((), (), s32[]{:S(2)}) async-start(), calls=%async_computation.3 | async-start | bytes 1114112 | tf_op jit(solution)/shard_map/all_gather | solution.py:42
  10.1 109.6 %reduce-scatter.4.cloned.1.call-start = ((), (), s32[]{:S(2)}) async-start(), calls=%async_computation.4 | async-start | bytes 1114112 | tf_op jit(solution)/shard_map/reduce_scatter | solution.py:46
  11.4 108.3 %copy-start.2 = (f32[128]{0:T(128)S(1)}, f32[128]{0:T(128)}, u32[]{:S(2)}) copy-start(f32[128]{0:T(128)} %param.10) | copy-start | bytes 1540
  50.3 8.1 %copy-start = (f32[1024,2048]{1,0:T(8,128)S(1)}, f32[1024,2048]{1,0:T(8,128)}, u32[]{:S(2)}) copy-start(f32[1024,2048]{1,0:T(8,128)} %param.7) | copy-start | bytes 25165828
  62.7 95.8 %all-gather.7.cloned.1.call-start = ((), (), s32[]{:S(2)}) async-start(), calls=%async_computation.5 | async-start | bytes 1114112 | tf_op jit(solution)/shard_map/all_gather | solution.py:42
  121.3 52.4 %copy-start.3 = (s32[128]{0:T(128)S(1)}, s32[128]{0:T(128)}, u32[]{:S(2)}) copy-start(s32[128]{0:T(128)} %param.13) | copy-start | bytes 1540
  121.3 53.6 %copy-start.1 = (s32[3,128]{1,0:T(4,128)S(1)}, s32[3,128]{1,0:T(4,128)}, u32[]{:S(2)}) copy-start(s32[3,128]{1,0:T(4,128)} %param.12) | copy-start | bytes 4612
  121.3 109.3 %reduce-scatter.6.cloned.1.call-start = ((), (), s32[]{:S(2)}) async-start(), calls=%async_computation.6 | async-start | bytes 1114112 | tf_op jit(solution)/shard_map/reduce_scatter | solution.py:46
  173.6 95.5 %all-gather.9.cloned.1.call-start = ((), (), s32[]{:S(2)}) async-start(), calls=%async_computation.7 | async-start | bytes 1114112 | tf_op jit(solution)/shard_map/all_gather | solution.py:42
  232.1 108.9 %reduce-scatter.8.cloned.1.call-start = ((), (), s32[]{:S(2)}) async-start(), calls=%async_computation.8 | async-start | bytes 1114112 | tf_op jit(solution)/shard_map/reduce_scatter | solution.py:46
  284.1 96.1 %all-gather.11.cloned.1.call-start = ((), (), s32[]{:S(2)}) async-start(), calls=%async_computation.9 | async-start | bytes 1114112 | tf_op jit(solution)/shard_map/all_gather | solution.py:42
Sparse Core Ops, SparseCore 0:
  10.7 39.4 all-gather.4
  62.8 56.8 reduce-scatter.3
  122.7 35.7 all-gather.6
  173.7 56.9 reduce-scatter.5
  233.2 35.8 all-gather.8
  284.2 56.8 reduce-scatter.7
  344.0 35.8 all-gather.10

commit v2 on v1

v2 whole, which is shorter than its diff:
```python
import functools

import jax
import jax.numpy as jnp
from jax import lax
from jax.experimental import pallas as pl
from jax.experimental.pallas import tpu as pltpu
from jax.sharding import PartitionSpec as P

OUTER = 2
INNER = 2
step_primal = 0.4
step_dual = 0.6
penalty = 1.0
MESH = pl.DeviceIdType.MESH
f32 = jnp.float32
bf16 = jnp.bfloat16


def split(value):
    high = value.astype(bf16)
    return high, (value - high.astype(f32)).astype(bf16)


def halves(wide):
    return wide[:, : wide.shape[1] // 2] + wide[:, wide.shape[1] // 2 :]


def kernel(
    n, total_cols,
    matrix, rhs, costs, upper, mask, node_map, weights,
    primal, dual, multipliers, gaps,
    staged, rows_cat, cols_cat, gathered, product, dual_cat, part, core_in, row_in, far_in,
    average, transposed, cap, averaging, gap_part, gap_all,
    load_sem, agz_s, agz_r, agy_s, agy_r, agc_s, agc_r, rsc_s, rsc_r, rsy_s, rsy_r, rsz_s, rsz_r, gap_s, gap_r,
):
    me = lax.axis_index("con")
    zs = n // 4
    z, y, c = me // 4, lax.rem(me // 2, 2), lax.rem(me, 2)
    width, scen = costs.shape
    rows = rhs.shape[0]
    chunk = 4 * width
    tile = 128

    def place(pz, py, pc):
        return pz * 4 + py * 2 + pc

    other_core, other_row = place(z, y, 1 - c), place(z, 1 - y, c)

    def remote(src, dst, send, recv, target):
        return pltpu.make_async_remote_copy(
            src_ref=src, dst_ref=dst, send_sem=send, recv_sem=recv,
            device_id={"con": target}, device_id_type=MESH,
        )

    def load(dz):
        at = lax.rem(z - dz + zs, zs)
        return pltpu.make_async_copy(
            matrix.at[:, pl.ds(pl.multiple_of(at * chunk, chunk), chunk)], staged.at[at], load_sem.at[dz]
        )

    for dz in range(zs):
        load(dz).start()

    barrier = pltpu.get_barrier_semaphore()
    for step in range(1, n):
        pl.semaphore_signal(barrier, inc=1, device_id={"con": lax.rem(me + step, n)}, device_id_type=MESH)

    bound = jnp.where(mask[...] > 0, upper[...], jnp.inf)
    cap[...] = jnp.transpose(jnp.broadcast_to(bound, (scen, width)))
    for ref in (primal, multipliers, average, transposed, dual, gap_part):
        ref[...] = jnp.zeros_like(ref)
    weight = weights[...].astype(f32)
    probability = weight / jnp.sum(weight)
    pl.semaphore_wait(barrier, n - 1)

    def prepare():
        by_row = jnp.transpose(jnp.broadcast_to(probability, (scen, scen)))
        for level in range(node_map.shape[0]):
            nodes = jnp.broadcast_to(node_map[pl.ds(level, 1), :].astype(f32), (scen, scen))
            mass = jnp.where(nodes == jnp.transpose(nodes), by_row, 0.0)
            averaging[level] = mass / jnp.sum(mass, axis=0, keepdims=True)

    def convert(dz):
        at = lax.rem(z - dz + zs, zs)
        load(dz).wait()

        @pl.loop(0, rows // tile)
        def _(step):
            here = pl.ds(pl.multiple_of(step * tile, tile), tile)
            block = staged[at, here, :]
            high, low = split(block)
            rows_cat[at, here, :chunk] = high
            rows_cat[at, here, chunk:] = low
            high, low = split(jnp.transpose(block))
            cols_cat[at, :, here] = high
            cols_cat[at, :, pl.ds(pl.multiple_of(rows + step * tile, tile), tile)] = low

    def agree(turn):
        now = primal[...]
        section = lax.rem(me * width + lax.broadcasted_iota(jnp.int32, now.shape, 0), averaging.shape[0] + 1)
        mean = now
        for level in range(averaging.shape[0]):
            at_level = jnp.dot(now, averaging[level], precision=lax.Precision.HIGHEST, preferred_element_type=f32)
            mean = jnp.where(section == level, at_level, mean)
        average[...] = mean
        deviation = now - mean
        multipliers[...] = multipliers[...] + penalty * deviation
        gap_part[pl.ds(turn, 1), :] = jnp.sum(deviation * deviation * probability, axis=0, keepdims=True)

    def gap_copy(step):
        return remote(gap_all.at[me], gap_all.at[me], gap_s.at[step], gap_r.at[step], lax.rem(me + step, n))

    last = OUTER * INNER - 1

    def one_pass(turn, carry):
        before = primal[...]
        prox = jnp.where(turn >= INNER, penalty, 0.0).astype(f32)
        gradient = costs[...] + multipliers[...] + prox * (before - average[...]) + transposed[...]
        moved = jnp.minimum(jnp.maximum(before - step_primal * gradient, 0.0), cap[...])
        primal[...] = moved
        gathered[me] = 2.0 * moved - before

        def slot_copy(slot, send, recv, target):
            copy = remote(gathered.at[slot], gathered.at[slot], send, recv, target)
            copy.start()
            return copy

        far, near, core = {}, {}, {}
        core[0, 0] = slot_copy(me, agc_s.at[0], agc_r.at[0], other_core)
        near[0] = slot_copy(me, agy_s.at[0], agy_r.at[0], other_row)
        for dz in range(1, zs):
            far[dz] = slot_copy(me, agz_s.at[dz], agz_r.at[dz], place(lax.rem(z + dz, zs), y, c))

        @pl.when(turn == 0)
        def _():
            prepare()

        @pl.when(lax.rem(turn, INNER) == INNER - 1)
        def _():
            agree(turn // INNER)

        @pl.when(turn == last)
        def _():
            gap_all[me] = gap_part[...]
            for step in range(1, n):
                gap_copy(step).start()

        def from_far(dz):
            if dz > 0:
                far[dz].wait_recv()
                slot = place(lax.rem(z - dz + zs, zs), y, c)
                near[dz] = slot_copy(slot, agy_s.at[dz], agy_r.at[dz], other_row)
                core[dz, 0] = slot_copy(slot, agc_s.at[2 * dz], agc_r.at[2 * dz], other_core)

        def from_near(dz):
            near[dz].wait_recv()
            slot = place(lax.rem(z - dz + zs, zs), 1 - y, c)
            core[dz, 1] = slot_copy(slot, agc_s.at[2 * dz + 1], agc_r.at[2 * dz + 1], other_core)

        def multiply(dz):
            at = lax.rem(z - dz + zs, zs)

            @pl.when(turn == 0)
            def _():
                convert(dz)

            core[dz, 0].wait_recv()
            core[dz, 1].wait_recv()
            arrived = gathered[pl.ds(at * 4, 4)].reshape(chunk, scen)
            wide = jnp.concatenate(split(arrived), axis=1)
            wide = jnp.concatenate([wide, wide], axis=0)
            term = halves(jnp.dot(rows_cat[at], wide, preferred_element_type=f32))
            if dz == 0:
                product[...] = term
            else:
                product[...] += term

        for dz in range(zs + 2):
            if dz < zs:
                from_far(dz)
            if 1 <= dz <= zs:
                from_near(dz - 1)
            if dz >= 2:
                multiply(dz - 2)
        for copy in [*far.values(), *near.values(), *core.values()]:
            copy.wait_send()

        now = jnp.maximum(dual[...] + step_dual * (product[...] - rhs[...]), 0.0)
        dual[...] = now

        @pl.when(turn < last)
        def _():
            wide = jnp.concatenate(split(now), axis=1)
            dual_cat[:rows] = wide
            dual_cat[rows:] = wide
            to_core, to_row, to_far = {}, {}, {}

            def transpose(dz):
                at = lax.rem(z + dz, zs)
                term = halves(jnp.dot(cols_cat[at], dual_cat[...], preferred_element_type=f32))
                part[pl.ds(at * 4, 4)] = term.reshape(4, width, scen)
                for k, py in enumerate((1 - y, y)):
                    index = 2 * dz + k
                    to_core[dz, k] = remote(
                        part.at[place(at, py, 1 - c)], core_in.at[index], rsc_s.at[index], rsc_r.at[index], other_core
                    )
                    to_core[dz, k].start()

            def add_core(dz):
                at = lax.rem(z + dz, zs)
                for k, py in enumerate((1 - y, y)):
                    to_core[dz, k].wait_recv()
                    slot = place(at, py, c)
                    part[slot] = part[slot] + core_in[2 * dz + k]
                    if k == 0:
                        to_row[dz] = remote(part.at[slot], row_in.at[dz], rsy_s.at[dz], rsy_r.at[dz], other_row)
                        to_row[dz].start()

            def add_row(dz):
                at = lax.rem(z + dz, zs)
                slot = place(at, y, c)
                to_row[dz].wait_recv()
                part[slot] = part[slot] + row_in[dz]
                if dz > 0:
                    to_far[dz] = remote(part.at[slot], far_in.at[dz], rsz_s.at[dz], rsz_r.at[dz], place(at, y, c))
                    to_far[dz].start()

            order = [*range(1, zs), 0]
            for step in range(zs + 2):
                if step < zs:
                    transpose(order[step])
                if 2 <= step:
                    add_row_at = step - 2
                else:
                    add_row_at = None
                if 1 <= step <= zs:
                    add_core(order[step - 1])
                if add_row_at is not None:
                    add_row(order[add_row_at])
            total = part[me]
            for dz in range(1, zs):
                to_far[dz].wait_recv()
                total = total + far_in[dz]
            transposed[...] = total
            for copy in [*to_core.values(), *to_row.values(), *to_far.values()]:
                copy.wait_send()

        return carry

    lax.fori_loop(0, last + 1, one_pass, 0)
    for step in range(1, n):
        gap_copy(step).wait_recv()
    everyone = jnp.sum(gap_all[...], axis=0)
    gaps[...] = jnp.broadcast_to(jnp.sum(everyone, axis=1, keepdims=True) / total_cols, gaps.shape)
    for step in range(1, n):
        gap_copy(step).wait_send()


def body(n, matrix, bounds_rhs, costs, upper, bound_mask, node_map, weights):
    rows, total_cols = matrix.shape
    width, scen = costs.shape
    zs = n // 4
    vmem = pl.BlockSpec(memory_space=pltpu.VMEM)
    dma = pltpu.SemaphoreType.DMA
    primal, dual, multipliers, gaps = pl.pallas_call(
        functools.partial(kernel, n, total_cols),
        out_shape=(
            jax.ShapeDtypeStruct((width, scen), f32),
            jax.ShapeDtypeStruct((rows, scen), f32),
            jax.ShapeDtypeStruct((width, scen), f32),
            jax.ShapeDtypeStruct((8, 128), f32),
        ),
        in_specs=[pl.BlockSpec(memory_space=pl.ANY)] + [vmem] * 6,
        out_specs=(vmem,) * 4,
        scratch_shapes=[
            pltpu.VMEM((zs, rows, 4 * width), f32),
            pltpu.VMEM((zs, rows, 8 * width), bf16),
            pltpu.VMEM((zs, 4 * width, 2 * rows), bf16),
            pltpu.VMEM((n, width, scen), f32),
            pltpu.VMEM((rows, scen), f32),
            pltpu.VMEM((2 * rows, 2 * scen), bf16),
            pltpu.VMEM((n, width, scen), f32),
            pltpu.VMEM((2 * zs, width, scen), f32),
            pltpu.VMEM((zs, width, scen), f32),
            pltpu.VMEM((zs, width, scen), f32),
            pltpu.VMEM((width, scen), f32),
            pltpu.VMEM((width, scen), f32),
            pltpu.VMEM((width, scen), f32),
            pltpu.VMEM((node_map.shape[0], scen, scen), f32),
            pltpu.VMEM((8, scen), f32),
            pltpu.VMEM((n, 8, scen), f32),
            dma((zs,)),
            dma((zs,)), dma((zs,)), dma((zs,)), dma((zs,)), dma((2 * zs,)), dma((2 * zs,)),
            dma((2 * zs,)), dma((2 * zs,)), dma((zs,)), dma((zs,)), dma((zs,)), dma((zs,)),
            dma((n,)), dma((n,)),
        ],
        compiler_params=pltpu.CompilerParams(collective_id=0, has_side_effects=True, vmem_limit_bytes=56 << 20),
    )(matrix, bounds_rhs, costs, upper[None, :], bound_mask[None, :], node_map, weights[None, :])
    return primal, dual, multipliers, gaps[:OUTER, 0]


def solution(mesh):
    placed = (
        P(("grp", "con"), None),
        P(("grp", "con"), None),
        P(("grp", "con"), None),
        P(("grp", "con")),
        P(("grp", "con")),
        P(None, "grp"),
        P("grp"),
    )
    return jax.shard_map(
        functools.partial(body, mesh.shape["con"]),
        mesh=mesh,
        in_specs=placed,
        out_specs=(
            P(("grp", "con"), None),
            P(("grp", "con"), None),
            P(("grp", "con"), None),
            P("grp"),
        ),
        check_vma=False,
    )
```

time: 397 us -> 123 us (0.31)
  waiting for transfers between devices: 281 us -> 0 us
  Pallas kernels: 0 us -> 116 us
  matrix products: 51.4 us -> 0 us
  blocking collectives: 31.6 us -> 0 us
  between operations: 15.6 us -> 0.64 us
  other arithmetic: 10.5 us -> 0 us
    reduce_scatter x3 -> x0, waiting for transfers between devices: 169 us -> none  [apply_columns(): lax.psum_scatter(lax.dot_general(matrix, dual, (((0,), (0,)), ((), ())),...]
    pallas_call x0 -> x1, Pallas kernels: none -> 116 us  [body(): pl.pallas_call(functools.partial(kernel, n, total_cols), out_shape=(jax.S...]
    all_gather x4 -> x0, waiting for transfers between devices: 112 us -> none  [apply_rows(): lax.all_gather(extrap, 'con', axis=0, tiled=True)]
    dot_general x9 -> x0, matrix products: 51.4 us -> none  [the longest x4 32 us: apply_rows(): jnp.dot(matrix, lax.all_gather(extrap, 'con', axis=0, tiled=True), precis...]
    psum x1 -> x0, blocking collectives: 31.6 us -> none  [body(): partial_value = lax.psum(partial_value, 'con')]
    sub x4 -> x0, other arithmetic: 4.51 us -> none  [the longest x3 4.51 us: body(): extrap = 2.0 * moved - primal]
  transfers between devices with their start and end apart: 7 -> 0, of which waited for: 6 -> 0; matrix products, arithmetic and copies ran while one was open for 2% -> 0% of each run, Pallas kernels for 0% -> 0%
where the time goes in v2:
time: 123 us; the launch traced here: 122 us
  Pallas kernels  116 us (94%)
  local copies, waits for them, and re-layouts  6.1 us (5%)
    pallas_call x1, Pallas kernels, body(): pl.pallas_call(functools.partial(kernel, n, total_cols), out_shape=(jax.S...  116 us
    unnamed x3, local copies, waits for them, and re-layouts  4.81 us

profile of v2, /device:TPU:0, one launch (start us, length us, event | category | flops | bytes accessed | tf_op | source)
XLA Modules:
  0.0 122.5 jit_solution(7686785279924364804)
XLA Ops:
  0.6 115.7 %shard_map.102 = (f32[128,128]{1,0:T(8,128)}, f32[1024,128]{1,0:T(8,128)}, f32[128,128]{1,0:T(8,128)}, f32[8,128]{1,0:T(8,128)}) custom-call(f32[1024,2048]{1,0:T(8,128)} %matrix.1, f32[1024,128]{1,0:T(8,128)} %rhs.2, f32[128,128]{1,0:T(8,128)} %costs.1, f32[1,128]{1,0:T(1,128)} %bitcast.3, s32[1,128]{1,0:T(1,128)} %bitcast.4, s32[3,128]{1,0:T(4,128)} %node_map.1, ...), custom_call_target="tpu_custom_call" | custom-call | tf_op jit(solution)/shard_map/pallas_call | solution.py:266
  116.4 1.3 %slice_reduce_fusion = f32[2]{0:T(128)} fusion(f32[8,128]{1,0:T(8,128)} %get-tuple-element.11), kind=kLoop, calls=%fused_computation | loop fusion | bytes 16 | tf_op jit(solution)/shard_map/slice | solution.py:300
  117.7 1.5 %copy.14 = f32[128,128]{1,0:T(8,128)} copy(f32[128,128]{1,0:T(8,128)} %get-tuple-element.16) | data formatting | bytes 131072
  119.1 1.9 %copy.15 = f32[1024,128]{1,0:T(8,128)} copy(f32[1024,128]{1,0:T(8,128)} %get-tuple-element.17) | data formatting | bytes 1048576
  121.0 1.5 %copy.16 = f32[128,128]{1,0:T(8,128)} copy(f32[128,128]{1,0:T(8,128)} %get-tuple-element.18) | data formatting | bytes 131072

commit v3 on v2

--- a/solution.py
+++ b/solution.py
@@ -24,6 +24,15 @@
 
 def halves(wide):
     return wide[:, : wide.shape[1] // 2] + wide[:, wide.shape[1] // 2 :]
+
+
+def across(z, step):
+    bit, partner = 1, z
+    while bit <= step:
+        if step & bit:
+            partner = partner + bit * (1 - 2 * lax.rem(z // bit, 2))
+        bit *= 2
+    return partner
 
 
 def kernel(
@@ -54,7 +63,7 @@
         )
 
     def load(dz):
-        at = lax.rem(z - dz + zs, zs)
+        at = across(z, dz)
         return pltpu.make_async_copy(
             matrix.at[:, pl.ds(pl.multiple_of(at * chunk, chunk), chunk)], staged.at[at], load_sem.at[dz]
         )
@@ -82,7 +91,7 @@
             averaging[level] = mass / jnp.sum(mass, axis=0, keepdims=True)
 
     def convert(dz):
-        at = lax.rem(z - dz + zs, zs)
+        at = across(z, dz)
         load(dz).wait()
 
         @pl.loop(0, rows // tile)
@@ -130,11 +139,12 @@
         core[0, 0] = slot_copy(me, agc_s.at[0], agc_r.at[0], other_core)
         near[0] = slot_copy(me, agy_s.at[0], agy_r.at[0], other_row)
         for dz in range(1, zs):
-            far[dz] = slot_copy(me, agz_s.at[dz], agz_r.at[dz], place(lax.rem(z + dz, zs), y, c))
+            far[dz] = slot_copy(me, agz_s.at[dz], agz_r.at[dz], place(across(z, dz), y, c))
 
         @pl.when(turn == 0)
         def _():
             prepare()
+            convert(0)
 
         @pl.when(lax.rem(turn, INNER) == INNER - 1)
         def _():
@@ -149,21 +159,23 @@
         def from_far(dz):
             if dz > 0:
                 far[dz].wait_recv()
-                slot = place(lax.rem(z - dz + zs, zs), y, c)
+                slot = place(across(z, dz), y, c)
                 near[dz] = slot_copy(slot, agy_s.at[dz], agy_r.at[dz], other_row)
                 core[dz, 0] = slot_copy(slot, agc_s.at[2 * dz], agc_r.at[2 * dz], other_core)
 
         def from_near(dz):
             near[dz].wait_recv()
-            slot = place(lax.rem(z - dz + zs, zs), 1 - y, c)
+            slot = place(across(z, dz), 1 - y, c)
             core[dz, 1] = slot_copy(slot, agc_s.at[2 * dz + 1], agc_r.at[2 * dz + 1], other_core)
 
         def multiply(dz):
-            at = lax.rem(z - dz + zs, zs)
-
-            @pl.when(turn == 0)
-            def _():
-                convert(dz)
+            at = across(z, dz)
+
+            if dz + 1 < zs:
+
+                @pl.when(turn == 0)
+                def _():
+                    convert(dz + 1)
 
             core[dz, 0].wait_recv()
             core[dz, 1].wait_recv()
@@ -176,13 +188,13 @@
             else:
                 product[...] += term
 
-        for dz in range(zs + 2):
-            if dz < zs:
-                from_far(dz)
-            if 1 <= dz <= zs:
-                from_near(dz - 1)
-            if dz >= 2:
-                multiply(dz - 2)
+        for dz in range(zs):
+            from_far(dz)
+        for dz in range(zs):
+            from_near(dz)
+            if dz >= 1:
+                multiply(dz - 1)
+        multiply(zs - 1)
         for copy in [*far.values(), *near.values(), *core.values()]:
             copy.wait_send()
 
@@ -197,7 +209,7 @@
             to_core, to_row, to_far = {}, {}, {}
 
             def transpose(dz):
-                at = lax.rem(z + dz, zs)
+                at = across(z, dz)
                 term = halves(jnp.dot(cols_cat[at], dual_cat[...], preferred_element_type=f32))
                 part[pl.ds(at * 4, 4)] = term.reshape(4, width, scen)
                 for k, py in enumerate((1 - y, y)):
@@ -208,7 +220,7 @@
                     to_core[dz, k].start()
 
             def add_core(dz):
-                at = lax.rem(z + dz, zs)
+                at = across(z, dz)
                 for k, py in enumerate((1 - y, y)):
                     to_core[dz, k].wait_recv()
                     slot = place(at, py, c)
@@ -218,7 +230,7 @@
                         to_row[dz].start()
 
             def add_row(dz):
-                at = lax.rem(z + dz, zs)
+                at = across(z, dz)
                 slot = place(at, y, c)
                 to_row[dz].wait_recv()
                 part[slot] = part[slot] + row_in[dz]
@@ -226,18 +238,14 @@
                     to_far[dz] = remote(part.at[slot], far_in.at[dz], rsz_s.at[dz], rsz_r.at[dz], place(at, y, c))
                     to_far[dz].start()
 
-            order = [*range(1, zs), 0]
-            for step in range(zs + 2):
+            order = [*range(zs - 1, -1, -1)]
+            for step in range(zs + 1):
                 if step < zs:
                     transpose(order[step])
-                if 2 <= step:
-                    add_row_at = step - 2
-                else:
-                    add_row_at = None
-                if 1 <= step <= zs:
+                if step >= 1:
                     add_core(order[step - 1])
-                if add_row_at is not None:
-                    add_row(order[add_row_at])
+            for dz in order:
+                add_row(dz)
             total = part[me]
             for dz in range(1, zs):
                 to_far[dz].wait_recv()
@@ -255,6 +263,14 @@
     gaps[...] = jnp.broadcast_to(jnp.sum(everyone, axis=1, keepdims=True) / total_cols, gaps.shape)
     for step in range(1, n):
         gap_copy(step).wait_send()
+
+
+def finish(primal_in, dual_in, multipliers_in, gaps_in, primal, dual, multipliers, gaps):
+    primal[...] = primal_in[...]
+    dual[...] = dual_in[...]
+    multipliers[...] = multipliers_in[...]
+    for turn in range(gaps.shape[0]):
+        gaps[turn] = jnp.max(gaps_in[pl.ds(turn, 1), :])
 
 
 def body(n, matrix, bounds_rhs, costs, upper, bound_mask, node_map, weights):
@@ -297,7 +313,17 @@
         ],
         compiler_params=pltpu.CompilerParams(collective_id=0, has_side_effects=True, vmem_limit_bytes=56 << 20),
     )(matrix, bounds_rhs, costs, upper[None, :], bound_mask[None, :], node_map, weights[None, :])
-    return primal, dual, multipliers, gaps[:OUTER, 0]
+    return pl.pallas_call(
+        finish,
+        out_shape=(
+            jax.ShapeDtypeStruct((width, scen), f32),
+            jax.ShapeDtypeStruct((rows, scen), f32),
+            jax.ShapeDtypeStruct((width, scen), f32),
+            jax.ShapeDtypeStruct((OUTER,), f32),
+        ),
+        in_specs=[vmem] * 4,
+        out_specs=(vmem, vmem, vmem, pl.BlockSpec(memory_space=pltpu.SMEM)),
+    )(primal, dual, multipliers, gaps)
 
 
 def solution(mesh):

time: 123 us -> 110 us (0.89)
  Pallas kernels: 116 us -> 109 us
  local copies, waits for them, and re-layouts: 6.1 us -> 0 us
    pallas_call x1, Pallas kernels: 116 us -> 107 us  [body(): pl.pallas_call(functools.partial(kernel, n, total_cols), out_shape=(jax.S...]
    unnamed x3 -> x0, local copies, waits for them, and re-layouts: 4.81 us -> none
    pallas_call x0 -> x1, Pallas kernels: none -> 1.92 us  [body(): pl.pallas_call(finish, out_shape=(jax.ShapeDtypeStruct((width, scen), f32...]
    slice x1 -> x0, local copies, waits for them, and re-layouts: 1.29 us -> none  [body(): return (primal, dual, multipliers, gaps[:OUTER, 0])]
where the time goes in v3:
time: 110 us
  Pallas kernels  109 us (99%)
    pallas_call x1, Pallas kernels, body(): pl.pallas_call(functools.partial(kernel, n, total_cols), out_shape=(jax.S...  107 us

profile of v3, /device:TPU:0, one launch (start us, length us, event | category | flops | bytes accessed | tf_op | source)
XLA Modules:
  0.0 109.6 jit_solution(16779063446631347720)
XLA Ops:
  0.6 107.0 %shard_map.102 = (f32[128,128]{1,0:T(8,128)}, f32[1024,128]{1,0:T(8,128)}, f32[128,128]{1,0:T(8,128)}, f32[8,128]{1,0:T(8,128)}) custom-call(f32[1024,2048]{1,0:T(8,128)} %matrix.1, f32[1024,128]{1,0:T(8,128)} %rhs.1, f32[128,128]{1,0:T(8,128)} %costs.1, f32[1,128]{1,0:T(1,128)} %bitcast.3, s32[1,128]{1,0:T(1,128)} %bitcast.4, s32[3,128]{1,0:T(4,128)} %node_map.1, ...), custom_call_target="tpu_custom_call" | custom-call | tf_op jit(solution)/shard_map/pallas_call | solution.py:282
  107.7 1.9 %shard_map.103 = (f32[128,128]{1,0:T(8,128)}, f32[1024,128]{1,0:T(8,128)}, f32[128,128]{1,0:T(8,128)}, f32[2]{0:T(128)}) custom-call(f32[128,128]{1,0:T(8,128)} %get-tuple-element.8.primal_in, f32[1024,128]{1,0:T(8,128)} %get-tuple-element.9.dual_in, f32[128,128]{1,0:T(8,128)} %get-tuple-element.10.multipliers_in, f32[8,128]{1,0:T(8,128)} %get-tuple-element.11.gaps_in), custom_call_target="tpu_custom_call" | custom-call | tf_op jit(solution)/shard_map/pallas_call | solution.py:316
